TPU v7x, 256 devices: a whole 4x4x8 slice. The times are simulated.
256 devices in a mesh: grp: 2 (over core), fsdp: 16 (over y, z_lo), tp: 8 (over x, z_hi).
Axes of the slice: x: 4, y: 4, z: 8 (z_hi: 2, z_lo: 4; z = z_hi * 4 + z_lo), core: 2. Of those that a mesh axis runs over, the one named last changes fastest.
Arguments:
- frames: bfloat16 [2, 4096, 8192], P('grp', 'fsdp'), may hold values from -6 to 6
- rewards: bfloat16 [4096], P('fsdp'), may hold values from -5 to 5
- actions: int32 [2, 4096], P('grp', 'fsdp'), may hold values from 0 to 17
- fractions: int32 [2, 4096, 32], P('grp', 'fsdp'), may hold values from 0 to 63
- episode_shard: int32 [4096, 1], P('fsdp'), may hold values from 0 to 15, as said below
- table: float32 [64], replicated, may hold values from 0.02 to 0.98
- norm_gain: float32 [8192], replicated, may hold values from 0.1 to 1.9
- torso_weight: bfloat16 [8192, 4096], P(('grp', 'fsdp'), 'tp'), may hold values from -0.0625 to 0.0625
- embed_weight: bfloat16 [64, 4096], P(None, 'tp'), may hold values from -0.75 to 0.75
- value_weight: bfloat16 [18, 4096], P(None, 'tp'), may hold values from -0.59765625 to 0.59765625
Outputs:
- torso_grad: float32 [8192, 4096], P(('grp', 'fsdp'), 'tp')
- refreshed_weight: bfloat16 [8192, 4096], P(('grp', 'fsdp', 'tp'))
Inputs may be any that keep to these rules, and one draw needn't show every extreme that they name: `episode_shard`: of the rows of one index of fsdp, at most 24 belong to one learner shard, and in every such block some learner shard gets exactly 24; every learner shard gets at least one row from every block.
All inputs are finite; a program needn't handle non-finite values.
Results may differ from a plain program's by a relative error of at most 0.0075.
Values may be sent and summed in bfloat16 or wider, within the bound.
No kernel may reach another device: no remote copies, remote signals or barrier semaphores. Data moves between devices by JAX's collectives and lax.ppermute only.
A program may use at most 64 MiB of HBM per device.

v0:
```python
import jax
import jax.numpy as jnp
from jax import lax
from jax.sharding import PartitionSpec as P

ACTIONS = 18
COSINES = 64
FRACS = 64


def shards(
    frames,
    rewards,
    actions,
    fractions,
    episode_shard,
    table,
    norm_gain,
    torso_weight,
    embed_weight,
    value_weight,
):
    shard_total = lax.axis_size("fsdp")
    destination = episode_shard[:, 0]
    rows_block = destination.shape[0]
    lanes = jnp.arange(shard_total, dtype=jnp.int32)
    onehot = (destination[:, None] == lanes[None, :]).astype(jnp.int32)
    counts = lax.psum(jnp.sum(onehot.astype(jnp.float32), axis=0), "fsdp")
    row_weight = jnp.dot(
        onehot.astype(jnp.float32), float(rows_block) / counts, precision=lax.Precision.HIGHEST
    )
    rows_data = frames[0]
    action_rows = actions[0]
    fraction_rows = fractions[0]
    values = rows_data.astype(jnp.float32)
    mean_square = jnp.mean(values * values, axis=-1, keepdims=True)
    normed = (values * lax.rsqrt(mean_square + 1e-05) * norm_gain).astype(jnp.bfloat16)
    columns = normed
    preact = jnp.dot(
        columns,
        lax.all_gather(torso_weight, ("grp", "fsdp"), axis=0, tiled=True),
        preferred_element_type=jnp.float32,
    )
    choose_mask = (action_rows[:, None] == jnp.arange(ACTIONS, dtype=jnp.int32)[None, :]).astype(
        jnp.bfloat16
    )
    picked = jnp.dot(choose_mask, value_weight, preferred_element_type=jnp.float32)
    weighted = (jax.nn.silu(preact) * picked).astype(jnp.bfloat16)
    cosine = jnp.cos(
        jnp.pi * jnp.arange(COSINES, dtype=jnp.float32)[None, :] * table[:, None]
    ).astype(jnp.bfloat16)
    embedding = jax.nn.relu(
        jnp.dot(cosine, embed_weight, preferred_element_type=jnp.float32)
    ).astype(jnp.bfloat16)
    table_values = lax.dot_general(
        weighted, embedding, (((1,), (1,)), ((), ())), preferred_element_type=jnp.float32
    )
    selector = (
        fraction_rows[:, :, None] == jnp.arange(FRACS, dtype=jnp.int32)[None, None, :]
    ).astype(jnp.float32)
    partial_quant = jnp.einsum(
        "mj,mtj->mt", table_values, selector, precision=lax.Precision.HIGHEST
    )
    group_index = lax.axis_index("grp")
    own_slot = jnp.arange(2, dtype=jnp.int32)[:, None, None] == group_index
    stacked = jnp.where(
        own_slot, partial_quant[None, :, :], jnp.zeros_like(partial_quant)[None, :, :]
    )
    summed = lax.psum(stacked, ("grp", "tp"))
    target_quant = summed[0]
    online_quant = summed[1]
    learner = (group_index == 1).astype(jnp.float32)
    levels = jnp.einsum("mtj,j->mt", selector, table, precision=lax.Precision.HIGHEST)
    target_value = rewards.astype(jnp.float32)[:, None] + 0.99 * target_quant
    errors = target_value[:, None, :] - online_quant[:, :, None]
    weight = jnp.abs(levels[:, :, None] - (errors < 0).astype(jnp.float32))
    grad_quant = -(learner * row_weight)[:, None] * jnp.sum(
        weight * jnp.clip(errors, -1.0, 1.0), axis=-1
    )
    grad_table = jnp.einsum("mi,mij->mj", grad_quant, selector, precision=lax.Precision.HIGHEST)
    grad_feature = jnp.dot(
        grad_table, embedding.astype(jnp.float32), precision=lax.Precision.HIGHEST
    )
    gate_value = jax.nn.sigmoid(preact)
    grad_preact = (grad_feature * picked * gate_value * (1.0 + preact * (1.0 - gate_value))).astype(
        jnp.bfloat16
    )
    columns = normed
    torso_grad = lax.psum_scatter(
        lax.dot_general(
            columns, grad_preact, (((0,), (0,)), ((), ())), preferred_element_type=jnp.float32
        ),
        ("grp", "fsdp"),
        scatter_dimension=0,
        tiled=True,
    )
    updated = (torso_weight.astype(jnp.float32) - 0.01 * torso_grad).astype(jnp.bfloat16)
    refreshed_weight = lax.all_to_all(updated, "tp", split_axis=0, concat_axis=1, tiled=True)
    return (torso_grad, refreshed_weight)


def solution(mesh):
    placed = (
        P("grp", "fsdp", None),
        P("fsdp"),
        P("grp", "fsdp"),
        P("grp", "fsdp", None),
        P("fsdp", None),
        P(),
        P(),
        P(("grp", "fsdp"), "tp"),
        P(None, "tp"),
        P(None, "tp"),
    )
    return jax.shard_map(
        shards,
        mesh=mesh,
        in_specs=placed,
        out_specs=(P(("grp", "fsdp"), "tp"), P(("grp", "fsdp", "tp"), None)),
        check_vma=False,
    )
```

profile of v0, /device:TPU:1, one launch (start us, length us, event | category | flops | bytes accessed | tf_op | source)
XLA Modules:
  0.0 676.3 jit_solution(3532035005112224799)
XLA Ops:
  7.2 0.0 copy-start
  7.2 0.0 all-gather.2.cloned.1.call-start
  7.3 0.7 all-gather.2.cloned.1.call-update
  8.0 0.0 all-reduce.2.cloned.1.call-start
  8.0 0.8 convert_reduce_fusion
  8.8 39.0 %psum.14 = f32[16]{0:T(128)S(1)} all-reduce(f32[16]{0:T(128)S(1)} %convert_reduce_fusion), channel_id=1, replica_groups=mesh['grp'=2,'fsdp'=16,'tp'=8] {'fsdp'}, use_global_device_ids=true, to_apply=%region_2.0 | all-reduce | flops 16 | bytes 128 | tf_op jit(solution)/shard_map/psum | solution.py:28
  47.8 3.2 fusion
  51.0 0.1 fusion.25
  51.1 0.0 copy-done.5
  51.1 0.3 fusion.12
  51.5 0.3 fusion.19
  51.7 3.8 fusion.15
  55.5 27.9 %all-gather.2.cloned.1.call-done = bf16[8192,512]{1,0:T(8,128)(2,1)} async-done(((bf16[256,512]{1,0:T(8,128)(2,1)}), bf16[8192,512]{1,0:T(8,128)(2,1)}) %all-gather.2.cloned.1.call-update) | async-done | bytes 8388624 | tf_op jit(solution)/shard_map/all_gather | solution.py:41
  83.4 7.0 %fusion.10 = f32[256,512]{1,0:T(8,128)S(1)} fusion(bf16[8192,512]{1,0:T(8,128)(2,1)} %all-gather.2.cloned.1.call-done, bf16[1,256,8192]{2,1,0:T(8,128)(2,1)} %param.10, f32[8192]{0:T(1024)S(1)} %copy-done.3, f32[256]{0:T(256)S(1)} %add_rsqrt_fusion), kind=kOutput, calls=%fused_computation.17 | convolution fusion | flops 2155872256 | bytes 13140992 | tf_op jit(solution)/shard_map/dot_general | solution.py:39
  90.5 0.3 fusion.18
  90.8 0.4 select_reduce_fusion.1
  91.1 0.7 broadcast_select_fusion
  91.8 0.0 all-reduce.2.cloned.1.call-update
  91.9 0.0 reduce-scatter.2.cloned.1.call-start
  91.9 2.8 copy.17
  94.8 172.4 %all-reduce.2.cloned.1.call-done = f32[2,256,32]{1,2,0:T(8,128)} async-done(((f32[2,256,32]{1,2,0:T(8,128)}), f32[2,256,32]{1,2,0:T(8,128)}) %all-reduce.2.cloned.1.call-update) | async-done | bytes 65552 | tf_op jit(solution)/shard_map/psum | solution.py:69
  267.1 0.8 slice_bitcast_fusion
  267.9 0.8 fusion.22
  268.7 0.3 fusion.14
  269.0 0.4 select_reduce_fusion
  269.4 0.5 fusion.7
  270.0 10.4 %fusion.8 = f32[8192,512]{1,0:T(8,128)} fusion(bf16[256,512]{1,0:T(8,128)(2,1)S(1)} %fusion.7, bf16[1,256,8192]{2,1,0:T(8,128)(2,1)} %param.10, f32[8192]{0:T(1024)S(1)} %copy-done.3, f32[256]{0:T(256)S(1)} %add_rsqrt_fusion), kind=kOutput, calls=%fused_computation.16 | convolution fusion | flops 2155872256 | bytes 21267456 | tf_op jit(solution)/shard_map/dot_general | solution.py:90
  280.4 0.0 reduce-scatter.2.cloned.1.call-update
  280.4 370.4 %reduce-scatter.2.cloned.1.call-done = f32[256,512]{1,0:T(8,128)} async-done(((f32[8192,512]{1,0:T(8,128)}), f32[256,512]{1,0:T(8,128)}) %reduce-scatter.2.cloned.1.call-update) | async-done | bytes 524304 | tf_op jit(solution)/shard_map/reduce_scatter | solution.py:89
  650.8 1.1 subtract_convert_fusion
  651.9 17.1 %all_to_all.19 = bf16[8,32,512]{2,1,0:T(8,128)(2,1)S(1)} all-to-all(bf16[8,32,512]{2,1,0:T(8,128)(2,1)S(1)} %bitcast.39), channel_id=1, replica_groups=mesh['grp'=2,'fsdp'=16,'tp'=8] {'tp'}, dimensions={0} | all-to-all | bytes 524288 | tf_op jit(solution)/shard_map/all_to_all | solution.py:98
  669.0 0.7 copy.31
  (22 shorter events, 0.1 us)
Async XLA Ops:
  7.2 44.0 %copy-start = (bf16[64,512]{1,0:T(8,128)(2,1)S(1)}, bf16[64,512]{1,0:T(8,128)(2,1)}, u32[]{:S(2)}) copy-start(bf16[64,512]{1,0:T(8,128)(2,1)} %param.18) | copy-start | bytes 196612
  7.2 43.8 %copy-start.7 = (s32[256,1]{0,1:T(1,128)S(1)}, s32[256,1]{0,1:T(1,128)}, u32[]{:S(2)}) copy-start(s32[256,1]{0,1:T(1,128)} %param.14) | copy-start | bytes 3076
  7.2 43.9 %copy-start.5 = (f32[64]{0:T(128)S(1)}, f32[64]{0:T(128)}, u32[]{:S(2)}) copy-start(f32[64]{0:T(128)} %param.15) | copy-start | bytes 772
  7.2 44.2 %copy-start.4 = (bf16[18,512]{1,0:T(8,128)(2,1)S(1)}, bf16[18,512]{1,0:T(8,128)(2,1)}, u32[]{:S(2)}) copy-start(bf16[18,512]{1,0:T(8,128)(2,1)} %param.19) | copy-start | bytes 55300
  7.2 44.2 %copy-start.6 = (s32[1,256]{1,0:T(1,128)S(1)}, s32[1,256]{1,0:T(1,128)}, u32[]{:S(2)}) copy-start(s32[1,256]{1,0:T(1,128)} %param.12) | copy-start | bytes 3076
  7.2 44.5 %copy-start.2 = (s32[1,256,32]{1,2,0:T(8,128)S(1)}, s32[1,256,32]{1,2,0:T(8,128)}, u32[]{:S(2)}) copy-start(s32[1,256,32]{1,2,0:T(8,128)} %param.13) | copy-start | bytes 98308
  7.2 76.2 %all-gather.2.cloned.1.call-start = ((), (), s32[]{:S(2)}) async-start(), calls=%async_computation.2 | async-start | bytes 8650752 | tf_op jit(solution)/shard_map/all_gather | solution.py:41
  8.0 259.2 %all-reduce.2.cloned.1.call-start = ((), (), s32[]{:S(2)}) async-start(), calls=%async_computation.3 | async-start | bytes 131072 | tf_op jit(solution)/shard_map/psum | solution.py:69
  47.8 35.6 %copy-start.3 = (f32[8192]{0:T(1024)S(1)}, f32[8192]{0:T(1024)}, u32[]{:S(2)}) copy-start(f32[8192]{0:T(1024)} %param.16) | copy-start | bytes 98308
  55.5 36.4 %copy-start.8 = (bf16[256]{0:T(256)(128)(2,1)S(1)}, bf16[256]{0:T(256)(128)(2,1)}, u32[]{:S(2)}) copy-start(bf16[256]{0:T(256)(128)(2,1)} %param.11) | copy-start | bytes 1540
  91.9 558.9 %reduce-scatter.2.cloned.1.call-start = ((), (), s32[]{:S(2)}) async-start(), calls=%async_computation.4 | async-start | bytes 17301504 | tf_op jit(solution)/shard_map/reduce_scatter | solution.py:89
  280.4 370.4 %copy-start.1 = (bf16[256,512]{1,0:T(8,128)(2,1)S(1)}, bf16[256,512]{1,0:T(8,128)(2,1)}, u32[]{:S(2)}) copy-start(bf16[256,512]{1,0:T(8,128)(2,1)} %param.17) | copy-start | bytes 786436
Sparse Core Ops, SparseCore 0:
  9.9 73.4 all-gather.1
  92.0 175.1 all-reduce.1
  280.5 370.1 reduce-scatter.1
where the time goes:
time: 677 us; the launch traced here: 676 us
  waiting for transfers between devices  571 us (84%)
  blocking collectives  56.1 us (8%)
  matrix products  22.7 us (3%)
  between operations  13.9 us (2%)
  other arithmetic  7.65 us (1%)
    reduce_scatter x1, waiting for transfers between devices, shards(): lax.psum_scatter(lax.dot_general(columns, grad_preact, (((0,), (0,)), (()...  370 us
    psum x1, waiting for transfers between devices, shards(): summed = lax.psum(stacked, ('grp', 'tp'))  172 us
    psum x1, blocking collectives, shards(): counts = lax.psum(jnp.sum(onehot.astype(jnp.float32), axis=0), 'fsdp')  39 us
    all_gather x1, waiting for transfers between devices, shards(): lax.all_gather(torso_weight, ('grp', 'fsdp'), axis=0, tiled=True)  27.9 us
    all_to_all x1, blocking collectives, shards(): lax.all_to_all(updated, 'tp', split_axis=0, concat_axis=1, tiled=True)  17.1 us
  transfers between devices with their start and end apart: 3, of which 3 were waited for; matrix products, arithmetic and copies ran while one was open for 2% of the time, Pallas kernels for 0%

commit v1 on v0

--- a/solution.py
+++ b/solution.py
@@ -66,7 +66,7 @@
     stacked = jnp.where(
         own_slot, partial_quant[None, :, :], jnp.zeros_like(partial_quant)[None, :, :]
     )
-    summed = lax.psum(stacked, ("grp", "tp"))
+    summed = lax.psum(lax.psum(stacked, "grp"), "tp")
     target_quant = summed[0]
     online_quant = summed[1]
     learner = (group_index == 1).astype(jnp.float32)

time: 677 us -> 632 us (0.934)
  waiting for transfers between devices: 571 us -> 527 us
    psum x1 -> x2, waiting for transfers between devices: 172 us -> 128 us  [shards(): summed = lax.psum(lax.psum(stacked, 'grp'), 'tp')]
  transfers between devices with their start and end apart: 3 -> 4, of which waited for: 3 -> 4; matrix products, arithmetic and copies ran while one was open for 2% -> 2% of each run, Pallas kernels for 0% -> 0%
where the time goes in v1:
time: 632 us
  waiting for transfers between devices  527 us (83%)
  blocking collectives  55.9 us (9%)
  matrix products  22.8 us (4%)
  between operations  13.9 us (2%)
  other arithmetic  7.65 us (1%)
    reduce_scatter x1, waiting for transfers between devices, shards(): lax.psum_scatter(lax.dot_general(columns, grad_preact, (((0,), (0,)), (()...  371 us
    psum x2, waiting for transfers between devices, shards(): summed = lax.psum(lax.psum(stacked, 'grp'), 'tp')  128 us
    psum x1, blocking collectives, shards(): counts = lax.psum(jnp.sum(onehot.astype(jnp.float32), axis=0), 'fsdp')  39 us
    all_gather x1, waiting for transfers between devices, shards(): lax.all_gather(torso_weight, ('grp', 'fsdp'), axis=0, tiled=True)  27.9 us
    all_to_all x1, blocking collectives, shards(): lax.all_to_all(updated, 'tp', split_axis=0, concat_axis=1, tiled=True)  16.8 us
  transfers between devices with their start and end apart: 4, of which 4 were waited for; matrix products, arithmetic and copies ran while one was open for 2% of the time, Pallas kernels for 0%

profile of v1, /device:TPU:1, one launch (start us, length us, event | category | flops | bytes accessed | tf_op | source)
XLA Modules:
  0.0 631.7 jit_solution(3746044577615661818)
XLA Ops:
  7.2 0.0 all-gather.2.cloned.1.call-start
  7.3 0.7 all-gather.2.cloned.1.call-update
  8.0 0.0 all-reduce.3.cloned.1.call-start
  8.0 0.8 convert_reduce_fusion
  8.8 39.0 %psum.21 = f32[16]{0:T(128)S(1)} all-reduce(f32[16]{0:T(128)S(1)} %convert_reduce_fusion), channel_id=1, replica_groups=mesh['grp'=2,'fsdp'=16,'tp'=8] {'fsdp'}, use_global_device_ids=true, to_apply=%region_2.0 | all-reduce | flops 16 | bytes 128 | tf_op jit(solution)/shard_map/psum | solution.py:28
  47.9 3.2 fusion
  51.0 0.3 fusion.12
  51.4 0.3 fusion.19
  51.7 3.8 fusion.15
  55.4 27.9 %all-gather.2.cloned.1.call-done = bf16[8192,512]{1,0:T(8,128)(2,1)} async-done(((bf16[256,512]{1,0:T(8,128)(2,1)}), bf16[8192,512]{1,0:T(8,128)(2,1)}) %all-gather.2.cloned.1.call-update) | async-done | bytes 8388624 | tf_op jit(solution)/shard_map/all_gather | solution.py:41
  83.4 7.0 %fusion.10 = f32[256,512]{1,0:T(8,128)S(1)} fusion(bf16[8192,512]{1,0:T(8,128)(2,1)} %all-gather.2.cloned.1.call-done, bf16[1,256,8192]{2,1,0:T(8,128)(2,1)} %param.10, f32[8192]{0:T(1024)S(1)} %copy-done.3, f32[256]{0:T(256)S(1)} %add_rsqrt_fusion), kind=kOutput, calls=%fused_computation.17 | convolution fusion | flops 2155872256 | bytes 13140992 | tf_op jit(solution)/shard_map/dot_general | solution.py:39
  90.4 0.3 fusion.18
  90.7 0.4 select_reduce_fusion.1
  91.1 0.7 broadcast_select_fusion
  91.8 0.0 all-reduce.3.cloned.1.call-update
  91.8 0.0 all-reduce.5.cloned.1.call-start
  91.9 0.1 fusion.25
  92.0 28.0 %all-reduce.3.cloned.1.call-done = f32[2,256,32]{1,2,0:T(8,128)} async-done(((f32[2,256,32]{1,2,0:T(8,128)}), f32[2,256,32]{1,2,0:T(8,128)}) %all-reduce.3.cloned.1.call-update) | async-done | bytes 65552 | tf_op jit(solution)/shard_map/psum | solution.py:69
  119.9 0.0 all-reduce.5.cloned.1.call-update
  120.0 0.0 reduce-scatter.2.cloned.1.call-start
  120.0 2.8 copy.17
  122.9 99.8 %all-reduce.5.cloned.1.call-done = f32[2,256,32]{1,2,0:T(8,128)} async-done(((f32[2,256,32]{1,2,0:T(8,128)}), f32[2,256,32]{1,2,0:T(8,128)}) %all-reduce.5.cloned.1.call-update) | async-done | bytes 65552 | tf_op jit(solution)/shard_map/psum | solution.py:69
  222.7 0.8 slice_bitcast_fusion
  223.5 0.8 fusion.22
  224.2 0.3 fusion.14
  224.6 0.4 select_reduce_fusion
  225.0 0.5 fusion.7
  225.5 10.4 %fusion.8 = f32[8192,512]{1,0:T(8,128)} fusion(bf16[256,512]{1,0:T(8,128)(2,1)S(1)} %fusion.7, bf16[1,256,8192]{2,1,0:T(8,128)(2,1)} %param.10, f32[8192]{0:T(1024)S(1)} %copy-done.3, f32[256]{0:T(256)S(1)} %add_rsqrt_fusion), kind=kOutput, calls=%fused_computation.16 | convolution fusion | flops 2155872256 | bytes 21267456 | tf_op jit(solution)/shard_map/dot_general | solution.py:90
  236.0 370.6 %reduce-scatter.2.cloned.1.call-done = f32[256,512]{1,0:T(8,128)} async-done(((f32[8192,512]{1,0:T(8,128)}), f32[256,512]{1,0:T(8,128)}) %reduce-scatter.2.cloned.1.call-update) | async-done | bytes 524304 | tf_op jit(solution)/shard_map/reduce_scatter | solution.py:89
  606.5 1.1 subtract_convert_fusion
  607.6 16.8 %all_to_all.19 = bf16[8,32,512]{2,1,0:T(8,128)(2,1)S(1)} all-to-all(bf16[8,32,512]{2,1,0:T(8,128)(2,1)S(1)} %bitcast.39), channel_id=1, replica_groups=mesh['grp'=2,'fsdp'=16,'tp'=8] {'tp'}, dimensions={0} | all-to-all | bytes 524288 | tf_op jit(solution)/shard_map/all_to_all | solution.py:98
  624.5 0.7 copy.31
  (25 shorter events, 0.1 us)
Async XLA Ops:
  7.2 43.9 %copy-start = (bf16[64,512]{1,0:T(8,128)(2,1)S(1)}, bf16[64,512]{1,0:T(8,128)(2,1)}, u32[]{:S(2)}) copy-start(bf16[64,512]{1,0:T(8,128)(2,1)} %param.18) | copy-start | bytes 196612
  7.2 43.9 %copy-start.5 = (f32[64]{0:T(128)S(1)}, f32[64]{0:T(128)}, u32[]{:S(2)}) copy-start(f32[64]{0:T(128)} %param.15) | copy-start | bytes 772
  7.2 44.2 %copy-start.4 = (bf16[18,512]{1,0:T(8,128)(2,1)S(1)}, bf16[18,512]{1,0:T(8,128)(2,1)}, u32[]{:S(2)}) copy-start(bf16[18,512]{1,0:T(8,128)(2,1)} %param.19) | copy-start | bytes 55300
  7.2 44.2 %copy-start.6 = (s32[1,256]{1,0:T(1,128)S(1)}, s32[1,256]{1,0:T(1,128)}, u32[]{:S(2)}) copy-start(s32[1,256]{1,0:T(1,128)} %param.12) | copy-start | bytes 3076
  7.2 44.4 %copy-start.2 = (s32[1,256,32]{1,2,0:T(8,128)S(1)}, s32[1,256,32]{1,2,0:T(8,128)}, u32[]{:S(2)}) copy-start(s32[1,256,32]{1,2,0:T(8,128)} %param.13) | copy-start | bytes 98308
  7.2 76.2 %all-gather.2.cloned.1.call-start = ((), (), s32[]{:S(2)}) async-start(), calls=%async_computation.2 | async-start | bytes 8650752 | tf_op jit(solution)/shard_map/all_gather | solution.py:41
  8.0 112.0 %all-reduce.3.cloned.1.call-start = ((), (), s32[]{:S(2)}) async-start(), calls=%async_computation.3 | async-start | bytes 131072 | tf_op jit(solution)/shard_map/psum | solution.py:69
  47.9 35.5 %copy-start.3 = (f32[8192]{0:T(1024)S(1)}, f32[8192]{0:T(1024)}, u32[]{:S(2)}) copy-start(f32[8192]{0:T(1024)} %param.16) | copy-start | bytes 98308
  55.4 36.4 %copy-start.7 = (s32[256,1]{0,1:T(1,128)S(1)}, s32[256,1]{0,1:T(1,128)}, u32[]{:S(2)}) copy-start(s32[256,1]{0,1:T(1,128)} %param.14) | copy-start | bytes 3076
  55.4 64.6 %copy-start.8 = (bf16[256]{0:T(256)(128)(2,1)S(1)}, bf16[256]{0:T(256)(128)(2,1)}, u32[]{:S(2)}) copy-start(bf16[256]{0:T(256)(128)(2,1)} %param.11) | copy-start | bytes 1540
  91.8 130.9 %all-reduce.5.cloned.1.call-start = ((), (), s32[]{:S(2)}) async-start(), calls=%async_computation.4 | async-start | bytes 131072 | tf_op jit(solution)/shard_map/psum | solution.py:69
  120.0 486.6 %reduce-scatter.2.cloned.1.call-start = ((), (), s32[]{:S(2)}) async-start(), calls=%async_computation.5 | async-start | bytes 17301504 | tf_op jit(solution)/shard_map/reduce_scatter | solution.py:89
  235.9 370.6 %copy-start.1 = (bf16[256,512]{1,0:T(8,128)(2,1)S(1)}, bf16[256,512]{1,0:T(8,128)(2,1)}, u32[]{:S(2)}) copy-start(bf16[256,512]{1,0:T(8,128)(2,1)} %param.17) | copy-start | bytes 786436
Sparse Core Ops, SparseCore 0:
  9.9 73.4 all-gather.1
  91.9 27.9 all-reduce.2
  122.5 100.1 all-reduce.4
  236.1 370.3 reduce-scatter.1
